TPU v7x, 128 devices: a whole 4x4x4 slice. The times are simulated.
128 devices in a mesh: tile: 16 (over x, z_lo, core), col: 8 (over y, z_hi).
Axes of the slice: x: 4, y: 4, z: 4 (z_hi: 2, z_lo: 2; z = z_hi * 2 + z_lo), core: 2. Of those that a mesh axis runs over, the one named last changes fastest.
Arguments:
- u_velocity: float32 [8192, 4096], P('tile', 'col'), may hold values from -12 to 12
- v_velocity: float32 [8192, 4096], P('tile', 'col'), may hold values from -12 to 12
- ocean_mask: int32 [64, 32], P('tile', 'col'), may hold values from 0 to 1, as said below
- tile_owner: int32 [64, 32], P('tile', 'col'), may hold values from 0 to 15, as said below
- lower_edge_quarter_turns: int32 [16], replicated, may hold values from 0 to 3
Outputs:
- library: float32 [16, 8, 16, 16, 1024], P('tile', 'col')
- gram: float32 [16, 16], replicated
Inputs may be any that keep to these rules, and one draw needn't show every extreme that they name: `ocean_mask`: in every column of devices (4 x 4 tile blocks), at least one device has only ocean tiles. `tile_owner`: among the ocean tiles of one device at most 1 share an owner; the ocean tiles of one column of devices are spread over its 16 owners so that the owners' counts differ by at most one. Land tiles carry an owner that is not used.
All inputs are finite; a program needn't handle non-finite values.
Results may differ from a plain program's by a relative error of at most 0.00014.
Values sent between devices are 32-bit elements; how exact they have to be, the bound alone decides.
No kernel may reach another device: no remote copies, remote signals or barrier semaphores. Data moves between devices by JAX's collectives and lax.ppermute only.
A program may use at most 192 MiB of HBM per device.

v0:
```python
import jax
import jax.numpy as jnp
from jax import lax
from jax.sharding import PartitionSpec as P

PASSES = 8
KAPPA = 0.2


def with_halo(cells, sides, width):
    for axis, dim in sides:
        count = lax.axis_size(axis)
        head = lax.slice_in_dim(cells, 0, width, axis=dim)
        tail = lax.slice_in_dim(cells, cells.shape[dim] - width, cells.shape[dim], axis=dim)
        cells = jnp.concatenate(
            [
                lax.ppermute(tail, axis, [(i, (i + 1) % count) for i in range(count)]),
                cells,
                lax.ppermute(head, axis, [((i + 1) % count, i) for i in range(count)]),
            ],
            axis=dim,
        )
    return cells


def quarter(first, second, turns):
    cosine = jnp.where(turns == 0, 1.0, jnp.where(turns == 2, -1.0, 0.0)).astype(first.dtype)
    sine = jnp.where(turns == 1, 1.0, jnp.where(turns == 3, -1.0, 0.0)).astype(first.dtype)
    return (cosine * first - sine * second, sine * first + cosine * second)


def turn_rims(padded, width, k_top, k_bottom):
    top_u, top_v = quarter(padded[0, :width], padded[1, :width], k_top)
    low_u, low_v = quarter(padded[0, -width:], padded[1, -width:], k_bottom)
    upper = jnp.stack([top_u, top_v])
    lower = jnp.stack([low_u, low_v])
    return jnp.concatenate([upper, padded[:, width:-width], lower], axis=1)


def relax(padded):
    centre = padded[:, 1:-1, 1:-1]
    beside_all = (
        padded[:, :-2, 1:-1] + padded[:, 2:, 1:-1] + padded[:, 1:-1, :-2] + padded[:, 1:-1, 2:]
    )
    return centre + KAPPA * (beside_all - 4.0 * centre)


def derive(padded):
    first = padded[..., 0, :, :]
    second = padded[..., 1, :, :]
    u_part = first[..., 1:-1, 1:-1]
    v_part = second[..., 1:-1, 1:-1]
    u_dx = (first[..., 1:-1, 2:] - first[..., 1:-1, :-2]) * 0.5
    u_dy = (first[..., 2:, 1:-1] - first[..., :-2, 1:-1]) * 0.5
    v_dx = (second[..., 1:-1, 2:] - second[..., 1:-1, :-2]) * 0.5
    v_dy = (second[..., 2:, 1:-1] - second[..., :-2, 1:-1]) * 0.5
    return jnp.stack([u_part, v_part, v_dx - u_dy, u_dy + v_dx, u_dx - v_dy], axis=-3)


def make_terms(base):
    u_part = base[..., 0, :]
    v_part = base[..., 1, :]
    vort = base[..., 2, :]
    strain = base[..., 3, :]
    stretch = base[..., 4, :]
    listed = [
        u_part,
        v_part,
        vort,
        strain,
        stretch,
        vort * vort,
        vort * strain,
        vort * stretch,
        strain * strain,
        stretch * stretch,
        strain * stretch,
        u_part * vort,
        v_part * vort,
        u_part * strain,
        v_part * stretch,
        u_part * v_part,
    ]
    return jnp.stack(listed, axis=-2)


def to_tiles(field, grid_x, grid_y, side):
    leading = field.shape[:-2]
    shaped = field.reshape(leading + (grid_x, side, grid_y, side))
    shaped = jnp.swapaxes(shaped, -3, -2)
    return shaped.reshape(leading + (grid_x * grid_y, side * side))


def per_device(u_velocity, v_velocity, ocean_mask, tile_owner, lower_edge_quarter_turns):
    rows_tile = lax.axis_size("tile")
    here = lax.axis_index("tile")
    k_top = lower_edge_quarter_turns[here]
    k_bottom = (4 - lower_edge_quarter_turns[(here + 1) % rows_tile]) % 4
    field = jnp.stack([u_velocity, v_velocity])
    for step in range(PASSES):
        padded = with_halo(field, (("tile", 1), ("col", 2)), 1)
        field = relax(turn_rims(padded, 1, k_top, k_bottom))
    fine_rows, fine_cols = u_velocity.shape
    coarse = field.reshape(2, fine_rows // 4, 4, fine_cols // 4, 4).mean(axis=(2, 4))
    coarse_pad = with_halo(coarse, (("tile", 1), ("col", 2)), 1)
    coarse_pad = turn_rims(coarse_pad, 1, k_top, k_bottom)
    grid_x, grid_y = ocean_mask.shape
    side = coarse.shape[1] // grid_x
    starting_tile_set = jnp.swapaxes(to_tiles(derive(coarse_pad), grid_x, grid_y, side), 0, 1)
    live = ocean_mask.reshape(-1) == 1
    owners = tile_owner.reshape(-1)
    tiles = live.shape[0]
    slots = tiles // rows_tile
    local = jnp.arange(tiles, dtype=jnp.int32)
    same = (owners[:, None] == owners[None, :]) & live[None, :] & (local[None, :] < local[:, None])
    slot = jnp.sum(same.astype(jnp.int32), axis=1)
    target = jnp.arange(rows_tile * slots, dtype=jnp.int32)
    chosen_terms = (
        live[None, :]
        & (owners[None, :] == target[:, None] // slots)
        & (slot[None, :] == target[:, None] % slots)
    ).astype(jnp.float32)
    library = make_terms(
        lax.all_to_all(
            jnp.einsum(
                "vh,hsd->vsd", chosen_terms, starting_tile_set, precision=lax.Precision.HIGHEST
            ),
            "tile",
            split_axis=0,
            concat_axis=0,
            tiled=True,
        )
    )
    part = jnp.einsum("pnc,pmc->nm", library, library, precision=lax.Precision.HIGHEST)
    gram = lax.psum(part, ("tile", "col")) / (fine_rows // 4 * (fine_cols // 4))
    return (library[None, None], gram)


def solution(mesh):
    in_specs = (P("tile", "col"), P("tile", "col"), P("tile", "col"), P("tile", "col"), P())
    out_specs = (P("tile", "col", None, None, None), P())
    return jax.shard_map(
        per_device, mesh=mesh, in_specs=in_specs, out_specs=out_specs, check_vma=False
    )
```

profile of v0, /device:TPU:1, one launch (start us, length us, event | category | flops | bytes accessed | tf_op | source)
XLA Modules:
  0.0 374.1 jit_solution(4603771623657914441)
XLA Ops:
  1.6 3.1 collective-permute-start
  8.2 3.5 collective-permute-start.2
  12.0 2.5 collective-permute-start.3
  21.4 6.4 %fusion.45 = f32[2,512,512]{2,1,0:T(8,128)S(1)} fusion(f32[2,514,1]{2,1,0:T(8,128)} %copy-done.15, f32[2,1,512]{2,1,0:T(1,128)S(1)} %collective-permute-done.1, f32[2,1,512]{2,1,0:T(1,128)S(1)} %collective-permute-done, f32[1,512,512]{2,1,0:T(8,128)S(1)} %bitcast.34, f32[1,512,512]{2,1,0:T(8,128)S(1)} %bitcast.28, f32[2,514,1]{2,1,0:T(8,128)} %copy-done.13, ...), kind=kLoop, calls=%fused_computation.129 | loop fusion | flops 10485760 | bytes 6324288 | tf_op jit(solution)/shard_map/add | solution.py:45
  34.3 4.6 %collective-permute-start.7 = (f32[2,514,1]{1,0,2:T(2,128)S(1)}, f32[2,514,1]{1,0,2:T(2,128)S(1)}, u32[]{:S(2)}, u32[]{:S(2)}) collective-permute-start(f32[2,514,1]{1,0,2:T(2,128)S(1)} %copy.209), channel_id=1, source_target_pairs={{1,0},{2,1},{3,2},{4,3},{5,4},{6,5},{7,6},{0,7},{9,8},{10,9},{11,1... | collective-permute-start | bytes 12344 | tf_op jit(solution)/shard_map/ppermute | solution.py:19
  44.0 8.1 %fusion.39 = f32[2,512,512]{2,1,0:T(8,128)S(1)} fusion(f32[2,512,512]{2,1,0:T(8,128)} %copy-done.9, f32[2,514,1]{2,1,0:T(8,128)S(1)} %copy-done.16, f32[2,1,512]{2,1,0:T(1,128)S(1)} %collective-permute-done.5, f32[2,1,512]{2,1,0:T(1,128)S(1)} %collective-permute-done.4, f32[2,514,1]{2,1,0:T(8,128)} %copy-done.14, f32[2,512,514]{2,1,0:T(8,128)S(1)} %slice.600, ...), kind=kLoop, calls=%fused_computation.113 | loop fusion | flops 8912896 | bytes 6324288 | tf_op jit(solution)/shard_map/add | solution.py:45
  53.3 3.0 collective-permute-start.9
  59.6 3.8 %collective-permute-start.11 = (f32[2,514,1]{1,0,2:T(2,128)S(1)}, f32[2,514,1]{1,0,2:T(2,128)S(1)}, u32[]{:S(2)}, u32[]{:S(2)}) collective-permute-start(f32[2,514,1]{1,0,2:T(2,128)S(1)} %copy.215), channel_id=1, source_target_pairs={{1,0},{2,1},{3,2},{4,3},{5,4},{6,5},{7,6},{0,7},{9,8},{10,9},{11,1... | collective-permute-start | bytes 12344 | tf_op jit(solution)/shard_map/ppermute | solution.py:19
  66.1 5.0 %fusion.33 = f32[2,512,512]{2,1,0:T(8,128)S(1)} fusion(f32[2,512,512]{2,1,0:T(8,128)S(1)} %fusion.39, f32[2,514,1]{2,1,0:T(8,128)S(1)} %copy.217, f32[2,1,512]{2,1,0:T(1,128)S(1)} %collective-permute-done.9, f32[2,1,512]{2,1,0:T(1,128)S(1)} %collective-permute-done.8, f32[2,514,1]{2,1,0:T(8,128)S(1)} %copy.216, f32[2,512,514]{2,1,0:T(8,128)S(1)} %slice.603, ...), kind=kLoop, calls=%fused_computation.97 | loop fusion | flops 8912896 | bytes 6324288 | tf_op jit(solution)/shard_map/add | solution.py:45
  71.8 4.6 %collective-permute-start.13 = (f32[2,1,512]{2,1,0:T(1,128)S(1)}, f32[2,1,512]{2,1,0:T(1,128)S(1)}, u32[]{:S(2)}, u32[]{:S(2)}) collective-permute-start(f32[2,1,512]{2,1,0:T(1,128)S(1)} %get-tuple-element.85), channel_id=1, source_target_pairs={{8,0},{16,8},{24,16},{32,24},{40,32},{48,40},{56,48},{64,56},{72,6... | collective-permute-start | bytes 12296 | tf_op jit(solution)/shard_map/ppermute | solution.py:19
  79.9 3.6 collective-permute-start.15
  86.0 5.0 %fusion.27 = f32[2,512,512]{2,1,0:T(8,128)S(1)} fusion(f32[2,512,512]{2,1,0:T(8,128)S(1)} %copy-done.1, f32[2,514,1]{2,1,0:T(8,128)S(1)} %copy.223, f32[2,1,512]{2,1,0:T(1,128)S(1)} %collective-permute-done.13, f32[2,1,512]{2,1,0:T(1,128)S(1)} %collective-permute-done.12, f32[2,514,1]{2,1,0:T(8,128)S(1)} %copy.222, f32[2,512,514]{2,1,0:T(8,128)S(1)} %slice.606, ...), kind=kLoop, calls=%fused_computation.81 | loop fusion | flops 8912896 | bytes 6324288 | tf_op jit(solution)/shard_map/add | solution.py:45
  91.0 5.6 %collective-permute-start.17 = (f32[2,1,512]{2,1,0:T(1,128)S(1)}, f32[2,1,512]{2,1,0:T(1,128)S(1)}, u32[]{:S(2)}, u32[]{:S(2)}) collective-permute-start(f32[2,1,512]{2,1,0:T(1,128)S(1)} %get-tuple-element.83), channel_id=1, source_target_pairs={{8,0},{16,8},{24,16},{32,24},{40,32},{48,40},{56,48},{64,56},{72,6... | collective-permute-start | bytes 12296 | tf_op jit(solution)/shard_map/ppermute | solution.py:19
  97.9 2.7 collective-permute-start.18
  100.8 2.7 collective-permute-start.19
  106.4 5.0 %fusion.21 = f32[2,512,512]{2,1,0:T(8,128)S(1)} fusion(f32[2,512,512]{2,1,0:T(8,128)S(1)} %copy-done.3, f32[2,514,1]{2,1,0:T(8,128)S(1)} %copy.229, f32[2,1,512]{2,1,0:T(1,128)S(1)} %collective-permute-done.17, f32[2,1,512]{2,1,0:T(1,128)S(1)} %collective-permute-done.16, f32[2,514,1]{2,1,0:T(8,128)S(1)} %copy.228, f32[2,512,514]{2,1,0:T(8,128)S(1)} %slice.609, ...), kind=kLoop, calls=%fused_computation.65 | loop fusion | flops 8912896 | bytes 6324288 | tf_op jit(solution)/shard_map/add | solution.py:45
  111.5 5.8 %collective-permute-start.21 = (f32[2,1,512]{2,1,0:T(1,128)S(1)}, f32[2,1,512]{2,1,0:T(1,128)S(1)}, u32[]{:S(2)}, u32[]{:S(2)}) collective-permute-start(f32[2,1,512]{2,1,0:T(1,128)S(1)} %get-tuple-element.81), channel_id=1, source_target_pairs={{8,0},{16,8},{24,16},{32,24},{40,32},{48,40},{56,48},{64,56},{72,6... | collective-permute-start | bytes 12296 | tf_op jit(solution)/shard_map/ppermute | solution.py:19
  121.1 3.3 collective-permute-start.23
  127.2 5.0 %fusion.15 = f32[2,512,512]{2,1,0:T(8,128)S(1)} fusion(f32[2,512,512]{2,1,0:T(8,128)S(1)} %copy-done.5, f32[2,514,1]{2,1,0:T(8,128)S(1)} %copy.235, f32[2,1,512]{2,1,0:T(1,128)S(1)} %collective-permute-done.21, f32[2,1,512]{2,1,0:T(1,128)S(1)} %collective-permute-done.20, f32[2,514,1]{2,1,0:T(8,128)S(1)} %copy.234, f32[2,512,514]{2,1,0:T(8,128)S(1)} %slice.612, ...), kind=kLoop, calls=%fused_computation.49 | loop fusion | flops 8912896 | bytes 6324288 | tf_op jit(solution)/shard_map/add | solution.py:45
  132.3 5.8 %collective-permute-start.25 = (f32[2,1,512]{2,1,0:T(1,128)S(1)}, f32[2,1,512]{2,1,0:T(1,128)S(1)}, u32[]{:S(2)}, u32[]{:S(2)}) collective-permute-start(f32[2,1,512]{2,1,0:T(1,128)S(1)} %get-tuple-element.79), channel_id=1, source_target_pairs={{8,0},{16,8},{24,16},{32,24},{40,32},{48,40},{56,48},{64,56},{72,6... | collective-permute-start | bytes 12296 | tf_op jit(solution)/shard_map/ppermute | solution.py:19
  141.9 2.8 collective-permute-start.27
  149.0 4.9 %fusion.9 = f32[2,512,512]{2,1,0:T(8,128)S(1)} fusion(f32[2,512,512]{2,1,0:T(8,128)S(1)} %copy-done.8, f32[2,514,1]{2,1,0:T(8,128)S(1)} %copy.241, f32[2,1,512]{2,1,0:T(1,128)S(1)} %collective-permute-done.25, f32[2,1,512]{2,1,0:T(1,128)S(1)} %collective-permute-done.24, f32[2,514,1]{2,1,0:T(8,128)S(1)} %copy.240, f32[2,512,514]{2,1,0:T(8,128)S(1)} %slice.615, ...), kind=kLoop, calls=%fused_computation.33 | loop fusion | flops 8912896 | bytes 6324288 | tf_op jit(solution)/shard_map/add | solution.py:45
  154.1 5.8 %collective-permute-start.29 = (f32[2,1,512]{2,1,0:T(1,128)S(1)}, f32[2,1,512]{2,1,0:T(1,128)S(1)}, u32[]{:S(2)}, u32[]{:S(2)}) collective-permute-start(f32[2,1,512]{2,1,0:T(1,128)S(1)} %get-tuple-element.77), channel_id=1, source_target_pairs={{8,0},{16,8},{24,16},{32,24},{40,32},{48,40},{56,48},{64,56},{72,6... | collective-permute-start | bytes 12296 | tf_op jit(solution)/shard_map/ppermute | solution.py:19
  163.7 3.0 collective-permute-start.31
  169.6 5.9 %fusion.3 = f32[2,512,512]{2,1,0:T(8,128)} fusion(f32[2,512,512]{2,1,0:T(8,128)S(1)} %fusion.9, f32[2,514,1]{2,1,0:T(8,128)S(1)} %copy.247, f32[2,1,512]{2,1,0:T(1,128)S(1)} %collective-permute-done.29, f32[2,1,512]{2,1,0:T(1,128)S(1)} %collective-permute-done.28, f32[2,514,1]{2,1,0:T(8,128)S(1)} %copy.246, f32[2,512,514]{2,1,0:T(8,128)S(1)} %slice.618, ...), kind=kLoop, calls=%fused_computation.17 | loop fusion | flops 8912896 | bytes 6324288 | tf_op jit(solution)/shard_map/add | solution.py:45
  175.5 71.4 %reshape.326 = f32[2,128,4,128,4]{4,3,2,1,0:T(8,128)} reshape(f32[2,512,512]{2,1,0:T(8,128)} %fusion.3) | data formatting | bytes 4194304 | tf_op jit(solution)/shard_map/reshape | solution.py:104
  246.9 20.8 %reduce_sum.19 = f32[2,128,128]{2,1,0:T(8,128)S(1)} reduce(f32[2,128,4,128,4]{4,3,2,1,0:T(8,128)} %reshape.326, f32[]{:T(128)} %constant.89.clone.1), dimensions={2,4}, to_apply=%region_1.2 | reduce | flops 491520 | bytes 2228228 | tf_op jit(solution)/shard_map/reduce_sum | solution.py:104
  267.8 5.7 %collective-permute-start.33 = (f32[2,1,128]{2,1,0:T(1,128)S(1)}, f32[2,1,128]{2,1,0:T(1,128)S(1)}, u32[]{:S(2)}, u32[]{:S(2)}) collective-permute-start(f32[2,1,128]{2,1,0:T(1,128)S(1)} %get-tuple-element.113), channel_id=1, source_target_pairs={{8,0},{16,8},{24,16},{32,24},{40,32},{48,40},{56,48},{64,56},{72,6... | collective-permute-start | bytes 3080 | tf_op jit(solution)/shard_map/ppermute | solution.py:19
  274.4 4.0 %collective-permute-start.34 = (f32[2,130,1]{2,1,0:T(8,128)S(1)}, f32[2,130,1]{2,1,0:T(8,128)S(1)}, u32[]{:S(2)}, u32[]{:S(2)}) collective-permute-start(f32[2,130,1]{2,1,0:T(8,128)S(1)} %get-tuple-element.110), channel_id=1, source_target_pairs={{0,1},{1,2},{2,3},{3,4},{4,5},{5,6},{6,7},{7,0},{8,9},{9,10},{10,1... | collective-permute-start | bytes 3128 | tf_op jit(solution)/shard_map/ppermute | solution.py:17
  279.6 2.4 collective-permute-done.34
  286.9 18.4 %all_to_all.5 = f32[16,5,1024]{2,1,0:T(8,128)S(1)} all-to-all(f32[16,5,1024]{2,1,0:T(8,128)S(1)} %copy.251), channel_id=1, replica_groups=mesh['tile'=16,'col'=8] {'tile'}, dimensions={0} | all-to-all | bytes 655360 | tf_op jit(solution)/shard_map/all_to_all | solution.py:124
  308.6 64.7 %psum.7 = f32[16,16]{1,0:T(8,128)S(1)} all-reduce(f32[16,16]{1,0:T(8,128)S(1)} %convolution_bitcast_fusion), channel_id=1, replica_groups=mesh['tile'=16,'col'=8] {'tile','col'}, use_global_device_ids=true, to_apply=%region_2.3 | all-reduce | flops 256 | bytes 2048 | tf_op jit(solution)/shard_map/psum | solution.py:135
  (226 shorter events, 70.2 us)
Async XLA Ops:
  8.2 10.1 %collective-permute-start.2 = (f32[2,514,1]{1,0,2:T(2,128)S(1)}, f32[2,514,1]{1,0,2:T(2,128)S(1)}, u32[]{:S(2)}, u32[]{:S(2)}) collective-permute-start(f32[2,514,1]{1,0,2:T(2,128)S(1)} %copy.202), channel_id=1, source_target_pairs={{0,1},{1,2},{2,3},{3,4},{4,5},{5,6},{6,7},{7,0},{8,9},{9,10},{10,1... | collective-permute-start | bytes 12344 | tf_op jit(solution)/shard_map/ppermute | solution.py:17
  12.0 6.6 %collective-permute-start.3 = (f32[2,514,1]{1,0,2:T(2,128)S(1)}, f32[2,514,1]{1,0,2:T(2,128)S(1)}, u32[]{:S(2)}, u32[]{:S(2)}) collective-permute-start(f32[2,514,1]{1,0,2:T(2,128)S(1)} %copy.203), channel_id=1, source_target_pairs={{1,0},{2,1},{3,2},{4,3},{5,4},{6,5},{7,6},{0,7},{9,8},{10,9},{11,1... | collective-permute-start | bytes 12344 | tf_op jit(solution)/shard_map/ppermute | solution.py:19
  33.3 6.1 %collective-permute-start.6 = (f32[2,514,1]{1,0,2:T(2,128)S(1)}, f32[2,514,1]{1,0,2:T(2,128)S(1)}, u32[]{:S(2)}, u32[]{:S(2)}) collective-permute-start(f32[2,514,1]{1,0,2:T(2,128)S(1)} %copy.208), channel_id=1, source_target_pairs={{0,1},{1,2},{2,3},{3,4},{4,5},{5,6},{6,7},{7,0},{8,9},{9,10},{10,1... | collective-permute-start | bytes 12344 | tf_op jit(solution)/shard_map/ppermute | solution.py:17
  34.3 5.4 %collective-permute-start.7 = (f32[2,514,1]{1,0,2:T(2,128)S(1)}, f32[2,514,1]{1,0,2:T(2,128)S(1)}, u32[]{:S(2)}, u32[]{:S(2)}) collective-permute-start(f32[2,514,1]{1,0,2:T(2,128)S(1)} %copy.209), channel_id=1, source_target_pairs={{1,0},{2,1},{3,2},{4,3},{5,4},{6,5},{7,6},{0,7},{9,8},{10,9},{11,1... | collective-permute-start | bytes 12344 | tf_op jit(solution)/shard_map/ppermute | solution.py:19
  52.1 4.9 %collective-permute-start.8 = (f32[2,1,512]{2,1,0:T(1,128)S(1)}, f32[2,1,512]{2,1,0:T(1,128)S(1)}, u32[]{:S(2)}, u32[]{:S(2)}) collective-permute-start(f32[2,1,512]{2,1,0:T(1,128)S(1)} %get-tuple-element.86), channel_id=1, source_target_pairs={{0,8},{8,16},{16,24},{24,32},{32,40},{40,48},{48,56},{56,64},{64,7... | collective-permute-start | bytes 12296 | tf_op jit(solution)/shard_map/ppermute | solution.py:17
  53.3 3.8 %collective-permute-start.9 = (f32[2,1,512]{2,1,0:T(1,128)S(1)}, f32[2,1,512]{2,1,0:T(1,128)S(1)}, u32[]{:S(2)}, u32[]{:S(2)}) collective-permute-start(f32[2,1,512]{2,1,0:T(1,128)S(1)} %get-tuple-element.87), channel_id=1, source_target_pairs={{8,0},{16,8},{24,16},{32,24},{40,32},{48,40},{56,48},{64,56},{72,6... | collective-permute-start | bytes 12296 | tf_op jit(solution)/shard_map/ppermute | solution.py:19
  57.6 6.6 %collective-permute-start.10 = (f32[2,514,1]{1,0,2:T(2,128)S(1)}, f32[2,514,1]{1,0,2:T(2,128)S(1)}, u32[]{:S(2)}, u32[]{:S(2)}) collective-permute-start(f32[2,514,1]{1,0,2:T(2,128)S(1)} %copy.214), channel_id=1, source_target_pairs={{0,1},{1,2},{2,3},{3,4},{4,5},{5,6},{6,7},{7,0},{8,9},{9,10},{10,1... | collective-permute-start | bytes 12344 | tf_op jit(solution)/shard_map/ppermute | solution.py:17
  59.6 4.8 %collective-permute-start.11 = (f32[2,514,1]{1,0,2:T(2,128)S(1)}, f32[2,514,1]{1,0,2:T(2,128)S(1)}, u32[]{:S(2)}, u32[]{:S(2)}) collective-permute-start(f32[2,514,1]{1,0,2:T(2,128)S(1)} %copy.215), channel_id=1, source_target_pairs={{1,0},{2,1},{3,2},{4,3},{5,4},{6,5},{7,6},{0,7},{9,8},{10,9},{11,1... | collective-permute-start | bytes 12344 | tf_op jit(solution)/shard_map/ppermute | solution.py:19
  71.1 5.9 %collective-permute-start.12 = (f32[2,1,512]{2,1,0:T(1,128)S(1)}, f32[2,1,512]{2,1,0:T(1,128)S(1)}, u32[]{:S(2)}, u32[]{:S(2)}) collective-permute-start(f32[2,1,512]{2,1,0:T(1,128)S(1)} %get-tuple-element.84), channel_id=1, source_target_pairs={{0,8},{8,16},{16,24},{24,32},{32,40},{40,48},{48,56},{56,64},{64,7... | collective-permute-start | bytes 12296 | tf_op jit(solution)/shard_map/ppermute | solution.py:17
  71.8 5.4 %collective-permute-start.13 = (f32[2,1,512]{2,1,0:T(1,128)S(1)}, f32[2,1,512]{2,1,0:T(1,128)S(1)}, u32[]{:S(2)}, u32[]{:S(2)}) collective-permute-start(f32[2,1,512]{2,1,0:T(1,128)S(1)} %get-tuple-element.85), channel_id=1, source_target_pairs={{8,0},{16,8},{24,16},{32,24},{40,32},{48,40},{56,48},{64,56},{72,6... | collective-permute-start | bytes 12296 | tf_op jit(solution)/shard_map/ppermute | solution.py:19
  77.7 6.4 %collective-permute-start.14 = (f32[2,514,1]{1,0,2:T(2,128)S(1)}, f32[2,514,1]{1,0,2:T(2,128)S(1)}, u32[]{:S(2)}, u32[]{:S(2)}) collective-permute-start(f32[2,514,1]{1,0,2:T(2,128)S(1)} %copy.220), channel_id=1, source_target_pairs={{0,1},{1,2},{2,3},{3,4},{4,5},{5,6},{6,7},{7,0},{8,9},{9,10},{10,1... | collective-permute-start | bytes 12344 | tf_op jit(solution)/shard_map/ppermute | solution.py:17
  79.9 4.4 %collective-permute-start.15 = (f32[2,514,1]{1,0,2:T(2,128)S(1)}, f32[2,514,1]{1,0,2:T(2,128)S(1)}, u32[]{:S(2)}, u32[]{:S(2)}) collective-permute-start(f32[2,514,1]{1,0,2:T(2,128)S(1)} %copy.221), channel_id=1, source_target_pairs={{1,0},{2,1},{3,2},{4,3},{5,4},{6,5},{7,6},{0,7},{9,8},{10,9},{11,1... | collective-permute-start | bytes 12344 | tf_op jit(solution)/shard_map/ppermute | solution.py:19
  90.9 6.3 %collective-permute-start.16 = (f32[2,1,512]{2,1,0:T(1,128)S(1)}, f32[2,1,512]{2,1,0:T(1,128)S(1)}, u32[]{:S(2)}, u32[]{:S(2)}) collective-permute-start(f32[2,1,512]{2,1,0:T(1,128)S(1)} %get-tuple-element.82), channel_id=1, source_target_pairs={{0,8},{8,16},{16,24},{24,32},{32,40},{40,48},{48,56},{56,64},{64,7... | collective-permute-start | bytes 12296 | tf_op jit(solution)/shard_map/ppermute | solution.py:17
  91.0 6.4 %collective-permute-start.17 = (f32[2,1,512]{2,1,0:T(1,128)S(1)}, f32[2,1,512]{2,1,0:T(1,128)S(1)}, u32[]{:S(2)}, u32[]{:S(2)}) collective-permute-start(f32[2,1,512]{2,1,0:T(1,128)S(1)} %get-tuple-element.83), channel_id=1, source_target_pairs={{8,0},{16,8},{24,16},{32,24},{40,32},{48,40},{56,48},{64,56},{72,6... | collective-permute-start | bytes 12296 | tf_op jit(solution)/shard_map/ppermute | solution.py:19
  97.9 6.3 %collective-permute-start.18 = (f32[2,514,1]{1,0,2:T(2,128)S(1)}, f32[2,514,1]{1,0,2:T(2,128)S(1)}, u32[]{:S(2)}, u32[]{:S(2)}) collective-permute-start(f32[2,514,1]{1,0,2:T(2,128)S(1)} %copy.226), channel_id=1, source_target_pairs={{0,1},{1,2},{2,3},{3,4},{4,5},{5,6},{6,7},{7,0},{8,9},{9,10},{10,1... | collective-permute-start | bytes 12344 | tf_op jit(solution)/shard_map/ppermute | solution.py:17
  100.8 4.0 %collective-permute-start.19 = (f32[2,514,1]{1,0,2:T(2,128)S(1)}, f32[2,514,1]{1,0,2:T(2,128)S(1)}, u32[]{:S(2)}, u32[]{:S(2)}) collective-permute-start(f32[2,514,1]{1,0,2:T(2,128)S(1)} %copy.227), channel_id=1, source_target_pairs={{1,0},{2,1},{3,2},{4,3},{5,4},{6,5},{7,6},{0,7},{9,8},{10,9},{11,1... | collective-permute-start | bytes 12344 | tf_op jit(solution)/shard_map/ppermute | solution.py:19
  111.4 6.4 %collective-permute-start.20 = (f32[2,1,512]{2,1,0:T(1,128)S(1)}, f32[2,1,512]{2,1,0:T(1,128)S(1)}, u32[]{:S(2)}, u32[]{:S(2)}) collective-permute-start(f32[2,1,512]{2,1,0:T(1,128)S(1)} %get-tuple-element.80), channel_id=1, source_target_pairs={{0,8},{8,16},{16,24},{24,32},{32,40},{40,48},{48,56},{56,64},{64,7... | collective-permute-start | bytes 12296 | tf_op jit(solution)/shard_map/ppermute | solution.py:17
  111.5 6.6 %collective-permute-start.21 = (f32[2,1,512]{2,1,0:T(1,128)S(1)}, f32[2,1,512]{2,1,0:T(1,128)S(1)}, u32[]{:S(2)}, u32[]{:S(2)}) collective-permute-start(f32[2,1,512]{2,1,0:T(1,128)S(1)} %get-tuple-element.81), channel_id=1, source_target_pairs={{8,0},{16,8},{24,16},{32,24},{40,32},{48,40},{56,48},{64,56},{72,6... | collective-permute-start | bytes 12296 | tf_op jit(solution)/shard_map/ppermute | solution.py:19
  118.6 6.1 %collective-permute-start.22 = (f32[2,514,1]{1,0,2:T(2,128)S(1)}, f32[2,514,1]{1,0,2:T(2,128)S(1)}, u32[]{:S(2)}, u32[]{:S(2)}) collective-permute-start(f32[2,514,1]{1,0,2:T(2,128)S(1)} %copy.232), channel_id=1, source_target_pairs={{0,1},{1,2},{2,3},{3,4},{4,5},{5,6},{6,7},{7,0},{8,9},{9,10},{10,1... | collective-permute-start | bytes 12344 | tf_op jit(solution)/shard_map/ppermute | solution.py:17
  121.1 4.5 %collective-permute-start.23 = (f32[2,514,1]{1,0,2:T(2,128)S(1)}, f32[2,514,1]{1,0,2:T(2,128)S(1)}, u32[]{:S(2)}, u32[]{:S(2)}) collective-permute-start(f32[2,514,1]{1,0,2:T(2,128)S(1)} %copy.233), channel_id=1, source_target_pairs={{1,0},{2,1},{3,2},{4,3},{5,4},{6,5},{7,6},{0,7},{9,8},{10,9},{11,1... | collective-permute-start | bytes 12344 | tf_op jit(solution)/shard_map/ppermute | solution.py:19
  132.2 6.4 %collective-permute-start.24 = (f32[2,1,512]{2,1,0:T(1,128)S(1)}, f32[2,1,512]{2,1,0:T(1,128)S(1)}, u32[]{:S(2)}, u32[]{:S(2)}) collective-permute-start(f32[2,1,512]{2,1,0:T(1,128)S(1)} %get-tuple-element.78), channel_id=1, source_target_pairs={{0,8},{8,16},{16,24},{24,32},{32,40},{40,48},{48,56},{56,64},{64,7... | collective-permute-start | bytes 12296 | tf_op jit(solution)/shard_map/ppermute | solution.py:17
  132.3 6.6 %collective-permute-start.25 = (f32[2,1,512]{2,1,0:T(1,128)S(1)}, f32[2,1,512]{2,1,0:T(1,128)S(1)}, u32[]{:S(2)}, u32[]{:S(2)}) collective-permute-start(f32[2,1,512]{2,1,0:T(1,128)S(1)} %get-tuple-element.79), channel_id=1, source_target_pairs={{8,0},{16,8},{24,16},{32,24},{40,32},{48,40},{56,48},{64,56},{72,6... | collective-permute-start | bytes 12296 | tf_op jit(solution)/shard_map/ppermute | solution.py:19
  139.3 6.1 %collective-permute-start.26 = (f32[2,514,1]{1,0,2:T(2,128)S(1)}, f32[2,514,1]{1,0,2:T(2,128)S(1)}, u32[]{:S(2)}, u32[]{:S(2)}) collective-permute-start(f32[2,514,1]{1,0,2:T(2,128)S(1)} %copy.238), channel_id=1, source_target_pairs={{0,1},{1,2},{2,3},{3,4},{4,5},{5,6},{6,7},{7,0},{8,9},{9,10},{10,1... | collective-permute-start | bytes 12344 | tf_op jit(solution)/shard_map/ppermute | solution.py:17
  141.9 4.0 %collective-permute-start.27 = (f32[2,514,1]{1,0,2:T(2,128)S(1)}, f32[2,514,1]{1,0,2:T(2,128)S(1)}, u32[]{:S(2)}, u32[]{:S(2)}) collective-permute-start(f32[2,514,1]{1,0,2:T(2,128)S(1)} %copy.239), channel_id=1, source_target_pairs={{1,0},{2,1},{3,2},{4,3},{5,4},{6,5},{7,6},{0,7},{9,8},{10,9},{11,1... | collective-permute-start | bytes 12344 | tf_op jit(solution)/shard_map/ppermute | solution.py:19
  154.0 6.4 %collective-permute-start.28 = (f32[2,1,512]{2,1,0:T(1,128)S(1)}, f32[2,1,512]{2,1,0:T(1,128)S(1)}, u32[]{:S(2)}, u32[]{:S(2)}) collective-permute-start(f32[2,1,512]{2,1,0:T(1,128)S(1)} %get-tuple-element.76), channel_id=1, source_target_pairs={{0,8},{8,16},{16,24},{24,32},{32,40},{40,48},{48,56},{56,64},{64,7... | collective-permute-start | bytes 12296 | tf_op jit(solution)/shard_map/ppermute | solution.py:17
  154.1 6.6 %collective-permute-start.29 = (f32[2,1,512]{2,1,0:T(1,128)S(1)}, f32[2,1,512]{2,1,0:T(1,128)S(1)}, u32[]{:S(2)}, u32[]{:S(2)}) collective-permute-start(f32[2,1,512]{2,1,0:T(1,128)S(1)} %get-tuple-element.77), channel_id=1, source_target_pairs={{8,0},{16,8},{24,16},{32,24},{40,32},{48,40},{56,48},{64,56},{72,6... | collective-permute-start | bytes 12296 | tf_op jit(solution)/shard_map/ppermute | solution.py:19
  161.1 6.1 %collective-permute-start.30 = (f32[2,514,1]{1,0,2:T(2,128)S(1)}, f32[2,514,1]{1,0,2:T(2,128)S(1)}, u32[]{:S(2)}, u32[]{:S(2)}) collective-permute-start(f32[2,514,1]{1,0,2:T(2,128)S(1)} %copy.244), channel_id=1, source_target_pairs={{0,1},{1,2},{2,3},{3,4},{4,5},{5,6},{6,7},{7,0},{8,9},{9,10},{10,1... | collective-permute-start | bytes 12344 | tf_op jit(solution)/shard_map/ppermute | solution.py:17
  163.7 4.3 %collective-permute-start.31 = (f32[2,514,1]{1,0,2:T(2,128)S(1)}, f32[2,514,1]{1,0,2:T(2,128)S(1)}, u32[]{:S(2)}, u32[]{:S(2)}) collective-permute-start(f32[2,514,1]{1,0,2:T(2,128)S(1)} %copy.245), channel_id=1, source_target_pairs={{1,0},{2,1},{3,2},{4,3},{5,4},{6,5},{7,6},{0,7},{9,8},{10,9},{11,1... | collective-permute-start | bytes 12344 | tf_op jit(solution)/shard_map/ppermute | solution.py:19
  267.7 6.3 %collective-permute-start.32 = (f32[2,1,128]{2,1,0:T(1,128)S(1)}, f32[2,1,128]{2,1,0:T(1,128)S(1)}, u32[]{:S(2)}, u32[]{:S(2)}) collective-permute-start(f32[2,1,128]{2,1,0:T(1,128)S(1)} %get-tuple-element.112), channel_id=1, source_target_pairs={{0,8},{8,16},{16,24},{24,32},{32,40},{40,48},{48,56},{56,64},{64,7... | collective-permute-start | bytes 3080 | tf_op jit(solution)/shard_map/ppermute | solution.py:17
  267.8 6.5 %collective-permute-start.33 = (f32[2,1,128]{2,1,0:T(1,128)S(1)}, f32[2,1,128]{2,1,0:T(1,128)S(1)}, u32[]{:S(2)}, u32[]{:S(2)}) collective-permute-start(f32[2,1,128]{2,1,0:T(1,128)S(1)} %get-tuple-element.113), channel_id=1, source_target_pairs={{8,0},{16,8},{24,16},{32,24},{40,32},{48,40},{56,48},{64,56},{72,6... | collective-permute-start | bytes 3080 | tf_op jit(solution)/shard_map/ppermute | solution.py:19
  274.4 7.6 %collective-permute-start.34 = (f32[2,130,1]{2,1,0:T(8,128)S(1)}, f32[2,130,1]{2,1,0:T(8,128)S(1)}, u32[]{:S(2)}, u32[]{:S(2)}) collective-permute-start(f32[2,130,1]{2,1,0:T(8,128)S(1)} %get-tuple-element.110), channel_id=1, source_target_pairs={{0,1},{1,2},{2,3},{3,4},{4,5},{5,6},{6,7},{7,0},{8,9},{9,10},{10,1... | collective-permute-start | bytes 3128 | tf_op jit(solution)/shard_map/ppermute | solution.py:17
  278.5 5.4 %collective-permute-start.35 = (f32[2,130,1]{2,1,0:T(8,128)S(1)}, f32[2,130,1]{2,1,0:T(8,128)S(1)}, u32[]{:S(2)}, u32[]{:S(2)}) collective-permute-start(f32[2,130,1]{2,1,0:T(8,128)S(1)} %get-tuple-element.111), channel_id=1, source_target_pairs={{1,0},{2,1},{3,2},{4,3},{5,4},{6,5},{7,6},{0,7},{9,8},{10,9},{11,1... | collective-permute-start | bytes 3128 | tf_op jit(solution)/shard_map/ppermute | solution.py:19
  (25 other events, 210.2 us)
where the time goes:
time: 381 us; the launch traced here: 374 us
  starting transfers between devices  91.9 us (24%)
  local copies, waits for them, and re-layouts  89.5 us (23%)
  blocking collectives  83.1 us (22%)
  other arithmetic  81.8 us (21%)
  waiting for transfers between devices  20.8 us (5%)
  between operations  5.18 us (1%)
    reshape x1, local copies, waits for them, and re-layouts, per_device(): field.reshape(2, fine_rows // 4, 4, fine_cols // 4, 4).mean(axis=(2, 4))  71.4 us
    psum x1, blocking collectives, per_device(): gram = lax.psum(part, ('tile', 'col')) / (fine_rows // 4 * (fine_cols // 4))  64.7 us
    ppermute x18, starting transfers between devices, with_halo(): lax.ppermute(head, axis, [((i + 1) % count, i) for i in range(count)])  64.6 us
    add x8, other arithmetic, relax(): return centre + KAPPA * (beside_all - 4.0 * centre)  45.1 us
    ppermute x18, starting transfers between devices, with_halo(): lax.ppermute(tail, axis, [(i, (i + 1) % count) for i in range(count)])  27.3 us
    reduce_sum x1, other arithmetic, per_device(): field.reshape(2, fine_rows // 4, 4, fine_cols // 4, 4).mean(axis=(2, 4))  20.8 us
    all_to_all x1, blocking collectives, per_device(): lax.all_to_all(jnp.einsum('vh,hsd->vsd', chosen_terms, starting_tile_set,...  18.4 us
    ppermute x18, waiting for transfers between devices, with_halo(): lax.ppermute(tail, axis, [(i, (i + 1) % count) for i in range(count)])  11.6 us
  transfers between devices with their start and end apart: 36, of which 31 were waited for; matrix products, arithmetic and copies ran while one was open for 1% of the time, Pallas kernels for 0%

commit v1 on v0

--- a/solution.py
+++ b/solution.py
@@ -132,7 +132,9 @@
         )
     )
     part = jnp.einsum("pnc,pmc->nm", library, library, precision=lax.Precision.HIGHEST)
-    gram = lax.psum(part, ("tile", "col")) / (fine_rows // 4 * (fine_cols // 4))
+    gram = jnp.sum(lax.all_gather(part, ("tile", "col")), axis=0) / (
+        fine_rows // 4 * (fine_cols // 4)
+    )
     return (library[None, None], gram)
 
 

time: 381 us -> 636 us (1.67)
  the two profiles are of different devices: /device:TPU:1 before, /device:TPU:0 now
where the time goes in v1:
time: 636 us; the launch traced here: 629 us
  blocking collectives  334 us (53%)
  local copies, waits for them, and re-layouts  89.5 us (14%)
  starting transfers between devices  88.6 us (14%)
  other arithmetic  81.9 us (13%)
  waiting for transfers between devices  28.3 us (4%)
    all_gather x1, blocking collectives, per_device(): lax.all_gather(part, ('tile', 'col'))  320 us
    reshape x1, local copies, waits for them, and re-layouts, per_device(): field.reshape(2, fine_rows // 4, 4, fine_cols // 4, 4).mean(axis=(2, 4))  71.4 us
    ppermute x18, starting transfers between devices, with_halo(): lax.ppermute(head, axis, [((i + 1) % count, i) for i in range(count)])  63.5 us
    add x8, other arithmetic, relax(): return centre + KAPPA * (beside_all - 4.0 * centre)  45.1 us
    ppermute x18, starting transfers between devices, with_halo(): lax.ppermute(tail, axis, [(i, (i + 1) % count) for i in range(count)])  25.1 us
    ppermute x18, waiting for transfers between devices, with_halo(): lax.ppermute(tail, axis, [(i, (i + 1) % count) for i in range(count)])  22.6 us
    reduce_sum x1, other arithmetic, per_device(): field.reshape(2, fine_rows // 4, 4, fine_cols // 4, 4).mean(axis=(2, 4))  20.8 us
    all_to_all x1, blocking collectives, per_device(): lax.all_to_all(jnp.einsum('vh,hsd->vsd', chosen_terms, starting_tile_set,...  14.1 us
  transfers between devices with their start and end apart: 36, of which 23 were waited for; matrix products, arithmetic and copies ran while one was open for 1% of the time, Pallas kernels for 0%

profile of v1, /device:TPU:0, one launch (start us, length us, event | category | flops | bytes accessed | tf_op | source)
XLA Modules:
  0.0 629.1 jit_solution(9926816217170332945)
XLA Ops:
  1.7 3.8 collective-permute-start.1
  7.3 4.0 collective-permute-start.2
  20.9 6.4 %fusion.45 = f32[2,512,512]{2,1,0:T(8,128)S(1)} fusion(f32[2,514,1]{2,1,0:T(8,128)} %copy-done.15, f32[2,1,512]{2,1,0:T(1,128)S(1)} %collective-permute-done.1, f32[2,1,512]{2,1,0:T(1,128)S(1)} %collective-permute-done, f32[1,512,512]{2,1,0:T(8,128)S(1)} %bitcast.35, f32[1,512,512]{2,1,0:T(8,128)S(1)} %bitcast.29, f32[2,514,1]{2,1,0:T(8,128)} %copy-done.13, ...), kind=kLoop, calls=%fused_computation.129 | loop fusion | flops 10485760 | bytes 6324288 | tf_op jit(solution)/shard_map/add | solution.py:45
  27.4 3.8 collective-permute-start.5
  36.2 4.8 collective-permute-start.7
  46.7 8.1 %fusion.39 = f32[2,512,512]{2,1,0:T(8,128)S(1)} fusion(f32[2,512,512]{2,1,0:T(8,128)} %copy-done.9, f32[2,514,1]{2,1,0:T(8,128)S(1)} %copy-done.16, f32[2,1,512]{2,1,0:T(1,128)S(1)} %collective-permute-done.5, f32[2,1,512]{2,1,0:T(1,128)S(1)} %collective-permute-done.4, f32[2,514,1]{2,1,0:T(8,128)} %copy-done.14, f32[2,512,514]{2,1,0:T(8,128)S(1)} %slice.600, ...), kind=kLoop, calls=%fused_computation.113 | loop fusion | flops 8912896 | bytes 6324288 | tf_op jit(solution)/shard_map/add | solution.py:45
  54.9 3.8 collective-permute-start.9
  62.8 3.8 collective-permute-start.11
  69.9 5.0 fusion.33
  74.9 3.8 collective-permute-start.13
  83.1 3.6 collective-permute-start.15
  90.1 5.0 fusion.27
  95.1 3.8 collective-permute-start.17
  100.8 2.9 collective-permute-start.18
  103.9 2.8 collective-permute-start.19
  110.7 5.0 fusion.21
  115.8 3.8 collective-permute-start.21
  124.2 3.6 collective-permute-start.23
  131.5 5.0 fusion.15
  136.6 3.8 collective-permute-start.25
  145.1 3.1 collective-permute-start.27
  153.3 4.9 fusion.9
  158.4 3.8 collective-permute-start.29
  166.8 3.3 collective-permute-start.31
  173.7 5.9 fusion.3
  179.7 71.4 %reshape.326 = f32[2,128,4,128,4]{4,3,2,1,0:T(8,128)} reshape(f32[2,512,512]{2,1,0:T(8,128)} %fusion.3) | data formatting | bytes 4194304 | tf_op jit(solution)/shard_map/reshape | solution.py:104
  251.1 20.8 %reduce_sum.28 = f32[2,128,128]{2,1,0:T(8,128)S(1)} reduce(f32[2,128,4,128,4]{4,3,2,1,0:T(8,128)} %reshape.326, f32[]{:T(128)} %constant.89.clone.1), dimensions={2,4}, to_apply=%region_1.2 | reduce | flops 491520 | bytes 2228228 | tf_op jit(solution)/shard_map/reduce_sum | solution.py:104
  272.0 3.8 collective-permute-start.33
  277.3 4.3 collective-permute-start.34
  283.0 3.0 collective-permute-done.34
  291.1 14.1 %all_to_all.5 = f32[16,5,1024]{2,1,0:T(8,128)S(1)} all-to-all(f32[16,5,1024]{2,1,0:T(8,128)S(1)} %copy.251), channel_id=1, replica_groups=mesh['tile'=16,'col'=8] {'tile'}, dimensions={0} | all-to-all | bytes 655360 | tf_op jit(solution)/shard_map/all_to_all | solution.py:124
  308.5 319.6 %all-gather = f32[2048,16]{1,0:T(8,128)S(1)} all-gather(f32[16,16]{1,0:T(8,128)S(1)} %convolution_bitcast_fusion), channel_id=2, replica_groups=mesh['tile'=16,'col'=8] {'tile','col'}, dimensions={0}, use_global_device_ids=true | all-gather | bytes 132096 | tf_op jit(solution)/shard_map/all_gather | solution.py:135
  (227 shorter events, 79.0 us)
Async XLA Ops:
  1.6 5.2 collective-permute-start
  7.3 10.6 %collective-permute-start.2 = (f32[2,514,1]{1,0,2:T(2,128)S(1)}, f32[2,514,1]{1,0,2:T(2,128)S(1)}, u32[]{:S(2)}, u32[]{:S(2)}) collective-permute-start(f32[2,514,1]{1,0,2:T(2,128)S(1)} %copy.202), channel_id=1, source_target_pairs={{0,1},{1,2},{2,3},{3,4},{4,5},{5,6},{6,7},{7,0},{8,9},{9,10},{10,1... | collective-permute-start | bytes 12344 | tf_op jit(solution)/shard_map/ppermute | solution.py:17
  11.5 6.6 %collective-permute-start.3 = (f32[2,514,1]{1,0,2:T(2,128)S(1)}, f32[2,514,1]{1,0,2:T(2,128)S(1)}, u32[]{:S(2)}, u32[]{:S(2)}) collective-permute-start(f32[2,514,1]{1,0,2:T(2,128)S(1)} %copy.203), channel_id=1, source_target_pairs={{1,0},{2,1},{3,2},{4,3},{5,4},{6,5},{7,6},{0,7},{9,8},{10,9},{11,1... | collective-permute-start | bytes 12344 | tf_op jit(solution)/shard_map/ppermute | solution.py:19
  27.3 5.2 collective-permute-start.4
  27.4 5.2 collective-permute-start.5
  34.8 7.3 %collective-permute-start.6 = (f32[2,514,1]{1,0,2:T(2,128)S(1)}, f32[2,514,1]{1,0,2:T(2,128)S(1)}, u32[]{:S(2)}, u32[]{:S(2)}) collective-permute-start(f32[2,514,1]{1,0,2:T(2,128)S(1)} %copy.208), channel_id=1, source_target_pairs={{0,1},{1,2},{2,3},{3,4},{4,5},{5,6},{6,7},{7,0},{8,9},{9,10},{10,1... | collective-permute-start | bytes 12344 | tf_op jit(solution)/shard_map/ppermute | solution.py:17
  36.2 6.2 collective-permute-start.7
  54.8 5.2 collective-permute-start.8
  54.9 5.2 collective-permute-start.9
  60.5 7.5 %collective-permute-start.10 = (f32[2,514,1]{1,0,2:T(2,128)S(1)}, f32[2,514,1]{1,0,2:T(2,128)S(1)}, u32[]{:S(2)}, u32[]{:S(2)}) collective-permute-start(f32[2,514,1]{1,0,2:T(2,128)S(1)} %copy.214), channel_id=1, source_target_pairs={{0,1},{1,2},{2,3},{3,4},{4,5},{5,6},{6,7},{7,0},{8,9},{9,10},{10,1... | collective-permute-start | bytes 12344 | tf_op jit(solution)/shard_map/ppermute | solution.py:17
  62.8 5.5 collective-permute-start.11
  74.8 5.2 collective-permute-start.12
  74.9 5.2 collective-permute-start.13
  80.6 7.3 %collective-permute-start.14 = (f32[2,514,1]{1,0,2:T(2,128)S(1)}, f32[2,514,1]{1,0,2:T(2,128)S(1)}, u32[]{:S(2)}, u32[]{:S(2)}) collective-permute-start(f32[2,514,1]{1,0,2:T(2,128)S(1)} %copy.220), channel_id=1, source_target_pairs={{0,1},{1,2},{2,3},{3,4},{4,5},{5,6},{6,7},{7,0},{8,9},{9,10},{10,1... | collective-permute-start | bytes 12344 | tf_op jit(solution)/shard_map/ppermute | solution.py:17
  83.1 5.4 collective-permute-start.15
  95.1 5.2 collective-permute-start.16
  95.1 5.2 collective-permute-start.17
  100.8 7.3 %collective-permute-start.18 = (f32[2,514,1]{1,0,2:T(2,128)S(1)}, f32[2,514,1]{1,0,2:T(2,128)S(1)}, u32[]{:S(2)}, u32[]{:S(2)}) collective-permute-start(f32[2,514,1]{1,0,2:T(2,128)S(1)} %copy.226), channel_id=1, source_target_pairs={{0,1},{1,2},{2,3},{3,4},{4,5},{5,6},{6,7},{7,0},{8,9},{9,10},{10,1... | collective-permute-start | bytes 12344 | tf_op jit(solution)/shard_map/ppermute | solution.py:17
  115.7 5.2 collective-permute-start.20
  115.8 5.2 collective-permute-start.21
  121.4 7.3 %collective-permute-start.22 = (f32[2,514,1]{1,0,2:T(2,128)S(1)}, f32[2,514,1]{1,0,2:T(2,128)S(1)}, u32[]{:S(2)}, u32[]{:S(2)}) collective-permute-start(f32[2,514,1]{1,0,2:T(2,128)S(1)} %copy.232), channel_id=1, source_target_pairs={{0,1},{1,2},{2,3},{3,4},{4,5},{5,6},{6,7},{7,0},{8,9},{9,10},{10,1... | collective-permute-start | bytes 12344 | tf_op jit(solution)/shard_map/ppermute | solution.py:17
  124.2 5.6 collective-permute-start.23
  136.5 5.2 collective-permute-start.24
  136.6 5.2 collective-permute-start.25
  142.2 7.3 %collective-permute-start.26 = (f32[2,514,1]{1,0,2:T(2,128)S(1)}, f32[2,514,1]{1,0,2:T(2,128)S(1)}, u32[]{:S(2)}, u32[]{:S(2)}) collective-permute-start(f32[2,514,1]{1,0,2:T(2,128)S(1)} %copy.238), channel_id=1, source_target_pairs={{0,1},{1,2},{2,3},{3,4},{4,5},{5,6},{6,7},{7,0},{8,9},{9,10},{10,1... | collective-permute-start | bytes 12344 | tf_op jit(solution)/shard_map/ppermute | solution.py:17
  158.3 5.2 collective-permute-start.28
  164.0 7.3 %collective-permute-start.30 = (f32[2,514,1]{1,0,2:T(2,128)S(1)}, f32[2,514,1]{1,0,2:T(2,128)S(1)}, u32[]{:S(2)}, u32[]{:S(2)}) collective-permute-start(f32[2,514,1]{1,0,2:T(2,128)S(1)} %copy.244), channel_id=1, source_target_pairs={{0,1},{1,2},{2,3},{3,4},{4,5},{5,6},{6,7},{7,0},{8,9},{9,10},{10,1... | collective-permute-start | bytes 12344 | tf_op jit(solution)/shard_map/ppermute | solution.py:17
  166.8 5.3 collective-permute-start.31
  271.9 5.3 collective-permute-start.32
  272.0 5.2 collective-permute-start.33
  277.3 8.7 %collective-permute-start.34 = (f32[2,130,1]{2,1,0:T(8,128)S(1)}, f32[2,130,1]{2,1,0:T(8,128)S(1)}, u32[]{:S(2)}, u32[]{:S(2)}) collective-permute-start(f32[2,130,1]{2,1,0:T(8,128)S(1)} %get-tuple-element.110), channel_id=1, source_target_pairs={{0,1},{1,2},{2,3},{3,4},{4,5},{5,6},{6,7},{7,0},{8,9},{9,10},{10,1... | collective-permute-start | bytes 3128 | tf_op jit(solution)/shard_map/ppermute | solution.py:17
  281.6 6.6 %collective-permute-start.35 = (f32[2,130,1]{2,1,0:T(8,128)S(1)}, f32[2,130,1]{2,1,0:T(8,128)S(1)}, u32[]{:S(2)}, u32[]{:S(2)}) collective-permute-start(f32[2,130,1]{2,1,0:T(8,128)S(1)} %get-tuple-element.111), channel_id=1, source_target_pairs={{1,0},{2,1},{3,2},{4,3},{5,4},{6,5},{7,6},{0,7},{9,8},{10,9},{11,1... | collective-permute-start | bytes 3128 | tf_op jit(solution)/shard_map/ppermute | solution.py:19
  (25 other events, 476.1 us)
